TPU v7x, 256 devices: a whole 4x4x8 slice. The times are simulated.
256 devices in a mesh: tok: 64 (over z, y, core), rep: 4 (over x).
Axes of the slice: x: 4, y: 4, z: 8, core: 2. Of those that a mesh axis runs over, the one named last changes fastest.
Arguments:
- patches: bfloat16 [65536, 768], P(('tok', 'rep')), may hold values from -6 to 6
- patch_view: int32 [65536], P(('tok', 'rep')), may hold values from 0 to 511
- rays: bfloat16 [65536, 768], P(('tok', 'rep')), may hold values from -24 to 24
- ray_view: int32 [65536], P(('tok', 'rep')), may hold values from 0 to 511
- targets: float32 [3, 65536], P(None, ('tok', 'rep')), may hold values from -6 to 6
- camera: bfloat16 [512, 768], P('tok'), may hold values from -6 to 6
- slots_init: float32 [64, 768], replicated, may hold values from -6 to 6
- key_weight: bfloat16 [768, 768], P('tok'), may hold values from -0.875 to 0.875
- value_weight: bfloat16 [768, 768], P('tok'), may hold values from -0.4375 to 0.4375
- query_weight: bfloat16 [768, 768], P('tok'), may hold values from -0.21875 to 0.21875
- gru_input: bfloat16 [768, 2304], P('tok'), may hold values from -0.21875 to 0.21875
- gru_hidden: bfloat16 [768, 2304], P('tok'), may hold values from -0.21875 to 0.21875
- mix_query: bfloat16 [768, 768], P('tok'), may hold values from -0.875 to 0.875
- mix_key: bfloat16 [768, 768], P('tok'), may hold values from -0.21875 to 0.21875
- render_in: bfloat16 [768, 1536], P('tok'), may hold values from -0.21875 to 0.21875
- render_out: bfloat16 [3, 1536], P(None, 'tok'), may hold values from -0.15625 to 0.15625
Outputs:
- slots_out: float32 [64, 768], replicated
- colour: float32 [3, 65536], P(None, ('tok', 'rep'))
- loss: float32 [], replicated
- grad_render_in: float32 [768, 1536], P('tok')
- grad_render_out: float32 [3, 1536], replicated
All inputs are finite; a program needn't handle non-finite values.
Results may differ from a plain program's by a relative error of at most 0.019.
Values may be sent and summed in bfloat16 or wider, within the bound.
A program may use at most 128 MiB of HBM per device.

v0:
```python
import jax
import jax.numpy as jnp
from jax import lax
from jax.sharding import Mesh
from jax.sharding import PartitionSpec as P

ITERS = 3
TOK = ("tok_0", "tok_1", "tok_2")
TOK_REP = ("tok_0", "tok_1", "tok_2", "rep")
EPSILON = 1e-05
ATTN_FLOOR = 1e-08


def from_everyone(value, axis):
    size = lax.axis_size(axis)
    return lax.all_to_all(
        jnp.broadcast_to(value[None], (size, *value.shape)), axis, 0, 0, tiled=True
    )


def in_order(parts, dim):
    parts = jnp.moveaxis(parts, 0, dim)
    lengths = parts.shape
    return parts.reshape(*lengths[:dim], lengths[dim] * lengths[dim + 1], *lengths[dim + 2 :])


def gathered_copies(value, axis, dim):
    parts = from_everyone(value, axis)
    return in_order(parts, dim)


def in_one_piece(arrays, axis, dim, along):
    both = jnp.concatenate(arrays, axis=along)
    filled, at, gathered = (lax.all_gather(both, axis, axis=dim, tiled=True), 0, [])
    for a in arrays:
        gathered.append(lax.slice_in_dim(filled, at, at + a.shape[along], axis=along))
        at += a.shape[along]
    return tuple(gathered)


def in_blocks(value, dim, size):
    lengths = value.shape
    parts = value.reshape(*lengths[:dim], size, lengths[dim] // size, *lengths[dim + 1 :])
    return jnp.moveaxis(parts, dim, 0)


def summed_on_arrival(value, axis, dim):
    size = lax.axis_size(axis)
    parts = lax.all_to_all(in_blocks(value, dim, size), axis, 0, 0, tiled=True)
    return jnp.sum(parts, axis=0)


def sum_in_two_steps(value, axes, dim):
    far, near = axes
    parts = in_blocks(value, dim, lax.axis_size(far))
    nearer = summed_on_arrival(parts, near, dim + 1)
    arrived = lax.all_to_all(nearer, far, split_axis=0, concat_axis=0, tiled=True)
    return arrived.sum(axis=0)


def padded_to(lines, size):
    spare = -lines.shape[0] % size
    if not spare:
        return lines
    return jnp.concatenate([lines, jnp.zeros((spare, *lines.shape[1:]), lines.dtype)])


def gather_axes(value, axes, dim):
    far, near = axes
    parts = from_everyone(from_everyone(value, far), near)
    return in_order(parts.swapaxes(0, 1).reshape(-1, *value.shape), dim)


def total_of(value, axes):
    own = sum_in_two_steps(
        padded_to(value, lax.axis_size(axes[0]) * lax.axis_size(axes[1])), axes, 0
    )
    whole = gather_axes(own, axes, 0)
    return whole[: len(value)].reshape(value.shape)


def packed_total(arrays, axis):
    vector, at, gathered = (jnp.concatenate([a.reshape(-1) for a in arrays]), 0, [])
    subtotal = total_of(vector, axis)
    for a in arrays:
        gathered.append(subtotal[at : at + a.size].reshape(a.shape))
        at += a.size
    return tuple(gathered)


def gather_in_order(value, axes, sequence):
    parts = value[None]
    for k in sequence:
        parts = lax.all_gather(parts, axes[k], axis=0, tiled=True)
    carried = [lax.axis_size(axes[k]) for k in reversed(sequence)]
    parts = parts.reshape(*carried, *value.shape)
    turned = sorted(range(len(sequence)), key=lambda place: sequence[len(sequence) - 1 - place])
    return parts.transpose(*turned, *range(len(sequence), parts.ndim)).reshape(-1, *value.shape)


def gather_axes_2(value, axes, sequence, dim):
    return in_order(gather_in_order(value, axes, sequence), dim)


def by_axis(value, axes):
    for axis in axes:
        value = lax.psum(value, axis)
    return value


def normalize(values):
    mean = jnp.mean(values, axis=-1, keepdims=True)
    centred = values - mean
    spread = jnp.mean(centred * centred, axis=-1, keepdims=True)
    return centred * lax.rsqrt(spread + EPSILON)


def lookup(table, index):
    onehot = (index[:, None] == jnp.arange(table.shape[0], dtype=jnp.int32)[None, :]).astype(
        jnp.bfloat16
    )
    return jnp.dot(onehot, table, preferred_element_type=jnp.float32)


def slot_update(slots, update, gru_input, gru_hidden):
    width = slots.shape[1]
    from_update = jnp.dot(
        update.astype(jnp.bfloat16), gru_input, preferred_element_type=jnp.float32
    )
    from_state = jnp.dot(slots.astype(jnp.bfloat16), gru_hidden, preferred_element_type=jnp.float32)
    reset = jax.nn.sigmoid(from_update[:, :width] + from_state[:, :width])
    blend = jax.nn.sigmoid(from_update[:, width : 2 * width] + from_state[:, width : 2 * width])
    candidate = jnp.tanh(from_update[:, 2 * width :] + reset * from_state[:, 2 * width :])
    return (1.0 - blend) * candidate + blend * slots


def add_rows(left, piece):
    return jnp.dot(left, piece, preferred_element_type=jnp.float32)


def on_device(
    patches,
    patch_view,
    rays,
    ray_view,
    targets,
    camera,
    slots_init,
    key_weight,
    value_weight,
    query_weight,
    gru_input,
    gru_hidden,
    mix_query,
    mix_key,
    render_in,
    render_out,
):
    width = patches.shape[1]
    scale = width ** (-0.5)
    table = gathered_copies(camera, TOK, 0)
    patch_in = patches.astype(jnp.float32) + lookup(table, patch_view)
    patch_x = normalize(patch_in).astype(jnp.bfloat16)
    pieces = in_one_piece((key_weight, value_weight), TOK, 0, 1)
    keys_sum = add_rows(patch_x, pieces[0])
    values_sum = add_rows(patch_x, pieces[1])
    keys = keys_sum.astype(jnp.bfloat16)
    values = values_sum.astype(jnp.bfloat16)
    query_full, input_full, hidden_full, mixkey_full, colour_full = (
        *in_one_piece((query_weight, gru_input, gru_hidden, mix_key), TOK, 0, 1),
        lax.all_gather(render_out, TOK, axis=1, tiled=True),
    )
    slots = slots_init
    for step in range(ITERS):
        query = (
            jnp.dot(
                normalize(slots).astype(jnp.bfloat16),
                query_full,
                preferred_element_type=jnp.float32,
            )
            * scale
        ).astype(jnp.bfloat16)
        logits = lax.dot_general(
            keys, query, (((1,), (1,)), ((), ())), preferred_element_type=jnp.float32
        )
        attn = jax.nn.softmax(logits, axis=1) + ATTN_FLOOR
        numer = lax.dot_general(
            attn.astype(jnp.bfloat16),
            values,
            (((0,), (0,)), ((), ())),
            preferred_element_type=jnp.float32,
        )
        denom = jnp.sum(attn, axis=0)
        numer, denom = packed_total((numer, denom), (("tok_0", "tok_1"), ("tok_2", "rep")))
        slots = slot_update(slots, numer / denom[:, None], input_full, hidden_full)
    slots_low = slots.astype(jnp.bfloat16)
    ray_in = rays.astype(jnp.float32) + lookup(table, ray_view)
    ray_x = ray_in.astype(jnp.bfloat16)
    ray_rows = ray_x.shape[0]
    query_sum = add_rows(ray_x, gather_axes_2(mix_query, TOK, (1, 0, 2), 0))
    ray_query = (query_sum * scale).astype(jnp.bfloat16)
    slot_keys = jnp.dot(slots_low, mixkey_full, preferred_element_type=jnp.float32).astype(
        jnp.bfloat16
    )
    mix_logits = lax.dot_general(
        ray_query, slot_keys, (((1,), (1,)), ((), ())), preferred_element_type=jnp.float32
    )
    mix = jax.nn.softmax(mix_logits, axis=1).astype(jnp.bfloat16)
    joined = (jnp.dot(mix, slots_low, preferred_element_type=jnp.float32) + ray_in).astype(
        jnp.bfloat16
    )
    pre = add_rows(joined, gather_axes(render_in, (("tok_0", "tok_1"), "tok_2"), 0))
    hidden = jax.nn.silu(pre).astype(jnp.bfloat16)
    colour = lax.dot_general(
        colour_full, hidden, (((1,), (1,)), ((), ())), preferred_element_type=jnp.float32
    )
    error = colour - targets
    rays_total = ray_rows * lax.axis_size(TOK) * lax.axis_size("rep")
    dcol = (error * (2.0 / jnp.sqrt(jnp.float32(3.0 * rays_total)))).astype(jnp.bfloat16)
    squared = jnp.sum(error * error)
    out_part = jnp.dot(dcol, hidden, preferred_element_type=jnp.float32)
    squared, grad_render_out = (by_axis(squared, TOK_REP), by_axis(out_part, TOK_REP))
    loss = squared / (3.0 * rays_total)
    dhidden = lax.dot_general(
        dcol, colour_full, (((0,), (0,)), ((), ())), preferred_element_type=jnp.float32
    )
    sig = jax.nn.sigmoid(pre)
    dpre = (dhidden * (sig + pre * sig * (1.0 - sig))).astype(jnp.bfloat16)
    mine = sum_in_two_steps(
        lax.dot_general(joined, dpre, (((0,), (0,)), ((), ())), preferred_element_type=jnp.float32),
        (("tok_0", "tok_1"), ("tok_2", "rep")),
        0,
    )
    grad_render_in = gathered_copies(mine, "rep", 0)
    return (slots, colour, loss, grad_render_in, grad_render_out)


def solution(mesh):
    torus = Mesh(
        mesh.devices.reshape(8, 4, 2, mesh.shape["rep"]), ("tok_0", "tok_1", "tok_2", "rep")
    )
    return jax.shard_map(
        on_device,
        mesh=torus,
        in_specs=(
            P(TOK_REP, None),
            P(TOK_REP),
            P(TOK_REP, None),
            P(TOK_REP),
            P(None, TOK_REP),
            P(TOK, None),
            P(),
            P(TOK, None),
            P(TOK, None),
            P(TOK, None),
            P(TOK, None),
            P(TOK, None),
            P(TOK, None),
            P(TOK, None),
            P(TOK, None),
            P(None, TOK),
        ),
        out_specs=(P(), P(None, TOK_REP), P(), P(TOK, None), P()),
        check_vma=False,
    )
```

profile of v0, /device:TPU:32, one launch (start us, length us, event | category | flops | bytes accessed | tf_op | source)
XLA Modules:
  0.0 691.2 jit_solution(10916712915491983667)
XLA Ops:
  13.0 11.8 %all-to-all-start = ((bf16[64,8,768]{2,1,0:T(8,128)(2,1)}), bf16[64,8,768]{2,1,0:T(8,128)(2,1)S(1)}, u32[]{:S(2)}, u32[]{:S(2)}) async-start(bf16[64,8,768]{2,1,0:T(8,128)(2,1)} %broadcast_in_dim.28), calls=%async_computation | async-start | bytes 1572864 | tf_op jit(solution)/shard_map/all_to_all | solution.py:16
  25.1 23.2 %all-to-all-done = bf16[64,8,768]{2,1,0:T(8,128)(2,1)S(1)} async-done(((bf16[64,8,768]{2,1,0:T(8,128)(2,1)}), bf16[64,8,768]{2,1,0:T(8,128)(2,1)S(1)}, u32[]{:S(2)}, u32[]{:S(2)}) %all-to-all-start) | async-done | bytes 786464 | tf_op jit(solution)/shard_map/all_to_all | solution.py:16
  49.0 43.4 %all-gather.11.cloned.1.call-done = bf16[64,12,1536]{2,1,0:T(8,128)(2,1)} async-done(((bf16[1,12,1536]{2,1,0:T(8,128)(2,1)}), bf16[64,12,1536]{2,1,0:T(8,128)(2,1)}) %all-gather.11.cloned.1.call-update) | async-done | bytes 2359312 | tf_op jit(solution)/shard_map/all_gather | solution.py:34
  92.4 4.9 reshape.143
  99.8 83.6 %all-gather.13.cloned.1.call-done = bf16[64,12,6144]{2,1,0:T(8,128)(2,1)} async-done(((bf16[1,12,6144]{2,1,0:T(8,128)(2,1)}), bf16[64,12,6144]{2,1,0:T(8,128)(2,1)}) %all-gather.13.cloned.1.call-update) | async-done | bytes 9437200 | tf_op jit(solution)/shard_map/all_gather | solution.py:34
  183.4 13.7 %reshape.145 = bf16[768,6144]{1,0:T(8,128)(2,1)} reshape(bf16[64,12,6144]{2,1,0:T(8,128)(2,1)} %all-gather.13.cloned.1.call-done) | data formatting | bytes 18874368
  199.9 10.9 %all_to_all.105 = f32[8,32,193]{2,1,0:T(8,128)S(1)} all-to-all(f32[8,32,193]{2,1,0:T(8,128)S(1)} %copy.54), channel_id=1, replica_groups=mesh['tok_0'=8,'tok_1'=4,'tok_2'=2,'rep'=4] {'tok_2','rep'}, dimensions={0} | all-to-all | bytes 395264 | tf_op jit(solution)/shard_map/all_to_all | solution.py:49
  210.9 14.4 %all_to_all.106 = f32[32,1,193]{2,1,0:T(1,128)S(1)} all-to-all(f32[32,1,193]{2,1,0:T(1,128)S(1)} %all_to_all.68), channel_id=1, replica_groups=mesh['tok_0'=8,'tok_1'=4,'tok_2'=2,'rep'=4] {'tok_0','tok_1'}, dimensions={0} | all-to-all | bytes 49408 | tf_op jit(solution)/shard_map/all_to_all | solution.py:57
  225.3 12.7 %all_to_all.107 = f32[32,1,193]{2,1,0:T(1,128)S(1)} all-to-all(f32[32,1,193]{2,1,0:T(1,128)S(1)} %broadcast_in_dim.29), channel_id=1, replica_groups=mesh['tok_0'=8,'tok_1'=4,'tok_2'=2,'rep'=4] {'tok_0','tok_1'}, dimensions={0} | all-to-all | bytes 49408 | tf_op jit(solution)/shard_map/all_to_all | solution.py:16
  238.8 3.4 all-to-all-start.4
  244.9 4.1 all-to-all-done.4
  249.6 2.8 fusion.9
  255.6 9.7 %all_to_all.108 = f32[8,32,193]{2,1,0:T(8,128)S(1)} all-to-all(f32[8,32,193]{2,1,0:T(8,128)S(1)} %copy.56), channel_id=1, replica_groups=mesh['tok_0'=8,'tok_1'=4,'tok_2'=2,'rep'=4] {'tok_2','rep'}, dimensions={0} | all-to-all | bytes 395264 | tf_op jit(solution)/shard_map/all_to_all | solution.py:49
  265.4 12.8 %all_to_all.109 = f32[32,1,193]{2,1,0:T(1,128)S(1)} all-to-all(f32[32,1,193]{2,1,0:T(1,128)S(1)} %all_to_all.73), channel_id=1, replica_groups=mesh['tok_0'=8,'tok_1'=4,'tok_2'=2,'rep'=4] {'tok_0','tok_1'}, dimensions={0} | all-to-all | bytes 49408 | tf_op jit(solution)/shard_map/all_to_all | solution.py:57
  278.3 12.7 %all_to_all.110 = f32[32,1,193]{2,1,0:T(1,128)S(1)} all-to-all(f32[32,1,193]{2,1,0:T(1,128)S(1)} %broadcast_in_dim.32), channel_id=1, replica_groups=mesh['tok_0'=8,'tok_1'=4,'tok_2'=2,'rep'=4] {'tok_0','tok_1'}, dimensions={0} | all-to-all | bytes 49408 | tf_op jit(solution)/shard_map/all_to_all | solution.py:16
  291.7 3.6 all-to-all-start.8
  298.0 3.9 all-to-all-done.8
  302.5 2.8 fusion.7
  308.7 9.9 %all_to_all.111 = f32[8,32,193]{2,1,0:T(8,128)} all-to-all(f32[8,32,193]{2,1,0:T(8,128)S(1)} %copy.58), channel_id=1, replica_groups=mesh['tok_0'=8,'tok_1'=4,'tok_2'=2,'rep'=4] {'tok_2','rep'}, dimensions={0} | all-to-all | bytes 395264 | tf_op jit(solution)/shard_map/all_to_all | solution.py:49
  319.9 5.0 all-to-all-start.13
  325.0 12.6 %all-gather.3 = bf16[4,12,768]{2,1,0:T(8,128)(2,1)S(1)} all-gather(bf16[1,12,768]{2,1,0:T(8,128)(2,1)S(1)} %bitcast.72), channel_id=2, replica_groups=mesh['tok_0'=8,'tok_1'=4,'tok_2'=2,'rep'=4] {'tok_1'}, dimensions={0}, use_global_device_ids=true | all-gather | bytes 92160 | tf_op jit(solution)/shard_map/all_gather | solution.py:94
  337.6 45.5 %all_gather.21 = bf16[32,12,768]{2,1,0:T(8,128)(2,1)S(1)} all-gather(bf16[4,12,768]{2,1,0:T(8,128)(2,1)S(1)} %all-gather.3), channel_id=1, replica_groups=mesh['tok_0'=8,'tok_1'=4,'tok_2'=2,'rep'=4] {'tok_0'}, dimensions={0}, use_global_device_ids=true | all-gather | bytes 663552 | tf_op jit(solution)/shard_map/all_gather | solution.py:94
  385.7 8.1 %all-to-all-start.10 = ((f32[32,1,193]{2,1,0:T(1,128)}), f32[32,1,193]{2,1,0:T(1,128)S(1)}, u32[]{:S(2)}, u32[]{:S(2)}) async-start(f32[32,1,193]{2,1,0:T(1,128)} %all_to_all.78), calls=%async_computation.10 | async-start | bytes 65536 | tf_op jit(solution)/shard_map/all_to_all | solution.py:57
  393.9 43.3 %all-gather.4 = bf16[64,24,3]{1,2,0:T(4,128)(2,1)S(1)} all-gather(bf16[1,24,3]{1,2,0:T(4,128)(2,1)S(1)} %bitcast.73), channel_id=1, replica_groups=mesh['tok_0'=8,'tok_1'=4,'tok_2'=2,'rep'=4] {'tok_0','tok_1','tok_2'}, dimensions={0}, use_global_device_ids=true | all-gather | bytes 9360 | tf_op jit(solution)/shard_map/all_gather | solution.py:171
  437.3 3.3 reshape.139
  440.6 3.1 copy.74
  443.7 3.1 reshape_reshape.33
  448.5 2.9 broadcast_in_dim.40
  451.4 3.9 all-to-all-start.14
  455.4 3.0 all-to-all-done.14
  459.1 8.2 %all-to-all-start.11 = ((f32[32,1,193]{2,1,0:T(1,128)}), f32[32,1,193]{2,1,0:T(1,128)S(1)}, u32[]{:S(2)}, u32[]{:S(2)}) async-start(f32[32,1,193]{2,1,0:T(1,128)} %broadcast_in_dim.35), calls=%async_computation.11 | async-start | bytes 65536 | tf_op jit(solution)/shard_map/all_to_all | solution.py:16
  469.6 3.0 copy.63
  476.8 3.6 all-to-all-start.12
  480.4 2.7 fusion
  483.2 3.8 all-to-all-done.12
  487.6 2.8 fusion.5
  493.4 3.6 fusion.31
  498.6 5.0 fusion.12
  503.6 7.9 %reshape_reshape.35 = f32[32,8,3,1536]{3,2,1,0:T(4,128)} reshape(f32[768,1536]{1,0:T(8,128)} %fusion.12) | data formatting | bytes 9437184 | tf_op jit(solution)/shard_map/reshape;reshape | solution.py:43
  511.5 5.5 copy.65
  517.0 57.9 %all_to_all.112 = f32[8,32,3,1536]{3,1,2,0:T(8,128)} all-to-all(f32[8,32,3,1536]{3,1,2,0:T(8,128)S(1)} %copy.65), channel_id=1, replica_groups=mesh['tok_0'=8,'tok_1'=4,'tok_2'=2,'rep'=4] {'tok_2','rep'}, dimensions={0} | all-to-all | bytes 9437184 | tf_op jit(solution)/shard_map/all_to_all | solution.py:49
  574.9 2.8 reduce_sum.238
  578.0 30.5 %all_to_all.113 = f32[32,3,1536]{2,1,0:T(4,128)S(1)} all-to-all(f32[32,3,1536]{2,1,0:T(4,128)S(1)} %copy.66), channel_id=1, replica_groups=mesh['tok_0'=8,'tok_1'=4,'tok_2'=2,'rep'=4] {'tok_0','tok_1'}, dimensions={0} | all-to-all | bytes 1179648 | tf_op jit(solution)/shard_map/all_to_all | solution.py:57
  609.3 3.3 all-to-all-start.17
  612.8 27.7 %all-reduce = (f32[]{:T(128)}, f32[3,1536]{1,0:T(4,128)S(1)}) all-reduce(f32[]{:T(128)} %get-tuple-element.18, f32[3,1536]{1,0:T(4,128)S(1)} %fusion.145), channel_id=1, replica_groups=mesh['tok_0'=8,'tok_1'=4,'tok_2'=2,'rep'=4] {'tok_0'}, use_global_device_ids=true, to_apply=%region_26.27 | all-reduce | flops 4609 | bytes 36872 | tf_op jit(solution)/shard_map/psum | solution.py:107
  640.6 17.6 %all-reduce.2 = (f32[]{:T(128)}, f32[3,1536]{1,0:T(4,128)S(1)}) all-reduce(f32[]{:T(128)} %get-tuple-element.5, f32[3,1536]{1,0:T(4,128)S(1)} %get-tuple-element.6), channel_id=1, replica_groups=mesh['tok_0'=8,'tok_1'=4,'tok_2'=2,'rep'=4] {'tok_1'}, use_global_device_ids=true, to_apply=%region_27.28 | all-reduce | flops 4609 | bytes 36872 | tf_op jit(solution)/shard_map/psum | solution.py:107
  658.2 4.5 all-reduce.3
  662.7 18.7 %all-reduce.1 = (f32[]{:T(128)}, f32[3,1536]{1,0:T(4,128)}) all-reduce(f32[]{:T(128)} %get-tuple-element.11, f32[3,1536]{1,0:T(4,128)S(1)} %get-tuple-element.12), channel_id=1, replica_groups=mesh['tok_0'=8,'tok_1'=4,'tok_2'=2,'rep'=4] {'rep'}, use_global_device_ids=true, to_apply=%region_29.30 | all-reduce | flops 4609 | bytes 36872 | tf_op jit(solution)/shard_map/psum | solution.py:107
  (138 shorter events, 46.2 us)
Async XLA Ops:
  8.0 16.7 %copy-start.3 = (f32[64,768]{1,0:T(8,128)S(1)}, f32[64,768]{1,0:T(8,128)}, u32[]{:S(2)}) copy-start(f32[64,768]{1,0:T(8,128)} %param.22) | copy-start | bytes 589828
  8.0 40.3 %copy-start.11 = (s32[256]{0:T(256)S(1)}, s32[256]{0:T(256)}, u32[]{:S(2)}) copy-start(s32[256]{0:T(256)} %param.17) | copy-start | bytes 3076
  8.0 40.2 %copy-start.6 = (bf16[256,768]{1,0:T(8,128)(2,1)S(1)}, bf16[256,768]{1,0:T(8,128)(2,1)}, u32[]{:S(2)}) copy-start(bf16[256,768]{1,0:T(8,128)(2,1)} %param.16) | copy-start | bytes 1179652
  8.0 84.4 %all-gather.11.cloned.1.call-start = ((), (), s32[]{:S(2)}) async-start(), calls=%async_computation.19 | async-start | bytes 3194880 | tf_op jit(solution)/shard_map/all_gather | solution.py:34
  9.6 173.8 %all-gather.13.cloned.1.call-start = ((), (), s32[]{:S(2)}) async-start(), calls=%async_computation.20 | async-start | bytes 12779520 | tf_op jit(solution)/shard_map/all_gather | solution.py:34
  13.0 35.3 %all-to-all-start = ((bf16[64,8,768]{2,1,0:T(8,128)(2,1)}), bf16[64,8,768]{2,1,0:T(8,128)(2,1)S(1)}, u32[]{:S(2)}, u32[]{:S(2)}) async-start(bf16[64,8,768]{2,1,0:T(8,128)(2,1)} %broadcast_in_dim.28), calls=%async_computation | async-start | bytes 1572864 | tf_op jit(solution)/shard_map/all_to_all | solution.py:16
  97.3 2.0 copy-start.4
  99.8 153.0 %copy-start.13 = (bf16[256,768]{1,0:T(8,128)(2,1)}, bf16[256,768]{1,0:T(8,128)(2,1)S(1)}, u32[]{:S(2)}) copy-start(bf16[256,768]{1,0:T(8,128)(2,1)S(1)} %convolution_convert_fusion.1) | copy-start | bytes 1179652
  238.8 10.2 %all-to-all-start.4 = ((f32[8,32,193]{2,1,0:T(8,128)}), f32[8,32,193]{2,1,0:T(8,128)S(1)}, u32[]{:S(2)}, u32[]{:S(2)}) async-start(f32[8,32,193]{2,1,0:T(8,128)} %broadcast_in_dim.31), calls=%async_computation.4 | async-start | bytes 524288 | tf_op jit(solution)/shard_map/all_to_all | solution.py:16
  291.7 10.2 %all-to-all-start.8 = ((f32[8,32,193]{2,1,0:T(8,128)}), f32[8,32,193]{2,1,0:T(8,128)S(1)}, u32[]{:S(2)}, u32[]{:S(2)}) async-start(f32[8,32,193]{2,1,0:T(8,128)} %broadcast_in_dim.34), calls=%async_computation.8 | async-start | bytes 524288 | tf_op jit(solution)/shard_map/all_to_all | solution.py:16
  305.8 12.8 %copy-start.7 = (bf16[12,1536]{1,0:T(8,128)(2,1)S(1)}, bf16[12,1536]{1,0:T(8,128)(2,1)}, u32[]{:S(2)}) copy-start(bf16[12,1536]{1,0:T(8,128)(2,1)} %param.30) | copy-start | bytes 110596
  318.6 6.4 copy-start.8
  319.9 65.8 %all-to-all-start.13 = ((bf16[32,12,1536]{2,1,0:T(8,128)(2,1)}), bf16[32,12,1536]{2,1,0:T(8,128)(2,1)S(1)}, u32[]{:S(2)}, u32[]{:S(2)}) async-start(bf16[32,12,1536]{2,1,0:T(8,128)(2,1)} %broadcast_in_dim.39), calls=%async_computation.13 | async-start | bytes 3145728 | tf_op jit(solution)/shard_map/all_to_all | solution.py:16
  324.9 68.9 %copy-start.12 = (bf16[3,24]{1,0:T(4,128)(2,1)S(1)}, bf16[3,24]{1,0:T(4,128)(2,1)}, u32[]{:S(2)}) copy-start(bf16[3,24]{1,0:T(4,128)(2,1)} %param.31) | copy-start | bytes 436
  324.9 112.4 %all-gather.9.cloned.1.call-start = ((), (), s32[]{:S(2)}) async-start(), calls=%async_computation.18 | async-start | bytes 1769472 | tf_op jit(solution)/shard_map/all_gather | solution.py:94
  385.7 62.8 %all-to-all-start.10 = ((f32[32,1,193]{2,1,0:T(1,128)}), f32[32,1,193]{2,1,0:T(1,128)S(1)}, u32[]{:S(2)}, u32[]{:S(2)}) async-start(f32[32,1,193]{2,1,0:T(1,128)} %all_to_all.78), calls=%async_computation.10 | async-start | bytes 65536 | tf_op jit(solution)/shard_map/all_to_all | solution.py:57
  451.4 15.9 %copy-start.10 = (s32[256]{0:T(256)S(1)}, s32[256]{0:T(256)}, u32[]{:S(2)}) copy-start(s32[256]{0:T(256)} %param.19) | copy-start | bytes 3076
  451.4 7.0 %all-to-all-start.14 = ((bf16[2,32,12,1536]{3,1,2,0:T(8,128)(2,1)}), bf16[2,32,12,1536]{3,1,2,0:T(8,128)(2,1)S(1)}, u32[]{:S(2)}, u32[]{:S(2)}) async-start(bf16[2,32,12,1536]{3,1,2,0:T(8,128)(2,1)} %broadcast_in_dim.40), calls=%async_computation.14 | async-start | bytes 4718592 | tf_op jit(solution)/shard_map/all_to_all | solution.py:16
  458.4 11.2 %copy-start = (bf16[2,32,12,1536]{3,1,2,0:T(8,128)(2,1)}, bf16[2,32,12,1536]{3,1,2,0:T(8,128)(2,1)S(1)}, u32[]{:S(2)}) copy-start(bf16[2,32,12,1536]{3,1,2,0:T(8,128)(2,1)S(1)} %all-to-all-done.14) | copy-start | bytes 7077892
  459.1 16.9 %all-to-all-start.11 = ((f32[32,1,193]{2,1,0:T(1,128)}), f32[32,1,193]{2,1,0:T(1,128)S(1)}, u32[]{:S(2)}, u32[]{:S(2)}) async-start(f32[32,1,193]{2,1,0:T(1,128)} %broadcast_in_dim.35), calls=%async_computation.11 | async-start | bytes 65536 | tf_op jit(solution)/shard_map/all_to_all | solution.py:16
  476.8 10.2 %all-to-all-start.12 = ((f32[8,32,193]{2,1,0:T(8,128)}), f32[8,32,193]{2,1,0:T(8,128)S(1)}, u32[]{:S(2)}, u32[]{:S(2)}) async-start(f32[8,32,193]{2,1,0:T(8,128)} %broadcast_in_dim.37), calls=%async_computation.12 | async-start | bytes 524288 | tf_op jit(solution)/shard_map/all_to_all | solution.py:16
  490.4 2.0 copy-start.1
  490.4 2.0 copy-start.2
  490.6 2.8 copy-start.5
  493.4 3.6 copy-start.9
  609.3 72.7 %all-to-all-start.17 = ((f32[4,3,1536]{2,1,0:T(4,128)}), f32[4,3,1536]{2,1,0:T(4,128)S(1)}, u32[]{:S(2)}, u32[]{:S(2)}) async-start(f32[4,3,1536]{2,1,0:T(4,128)} %broadcast_in_dim.41), calls=%async_computation.17 | async-start | bytes 196608 | tf_op jit(solution)/shard_map/all_to_all | solution.py:16
Sparse Core Ops, SparseCore 0:
  12.2 80.1 all-gather.10
  95.7 87.6 all-gather.12
Sparse Core Ops, SparseCore 1:
  384.2 11.9 all-gather.8
where the time goes:
time: 694 us; the launch traced here: 691 us
  blocking collectives  341 us (49%)
  waiting for transfers between devices  166 us (24%)
  local copies, waits for them, and re-layouts  64.1 us (9%)
  starting transfers between devices  51.1 us (7%)
  matrix products  41.2 us (6%)
  between operations  17.9 us (3%)
  other arithmetic  9.31 us (1%)
    all_gather x2, waiting for transfers between devices, in_one_piece(): lax.all_gather(both, axis, axis=dim, tiled=True)  127 us
    all_to_all x4, blocking collectives, summed_on_arrival(): parts = lax.all_to_all(in_blocks(value, dim, size), axis, 0, 0, tiled=True)  88.5 us
    psum x4, blocking collectives, by_axis(): value = lax.psum(value, axis)  68.5 us
    all_gather x2, blocking collectives, gather_in_order(): parts = lax.all_gather(parts, axes[k], axis=0, tiled=True)  58 us
    all_to_all x3, blocking collectives, sum_in_two_steps(): lax.all_to_all(nearer, far, split_axis=0, concat_axis=0, tiled=True)  57.7 us
    all_gather x1, blocking collectives, on_device(): lax.all_gather(render_out, TOK, axis=1, tiled=True)  43.3 us
    all_to_all x8, starting transfers between devices, from_everyone(): lax.all_to_all(jnp.broadcast_to(value[None], (size, *value.shape)), axis,...  42.8 us
    all_to_all x8, waiting for transfers between devices, from_everyone(): lax.all_to_all(jnp.broadcast_to(value[None], (size, *value.shape)), axis,...  39.3 us
  transfers between devices with their start and end apart: 12, of which 8 were waited for; matrix products, arithmetic and copies ran while one was open for 6% of the time, Pallas kernels for 0%

commit v1 on v0

--- a/solution.py
+++ b/solution.py
@@ -166,9 +166,16 @@
     values_sum = add_rows(patch_x, pieces[1])
     keys = keys_sum.astype(jnp.bfloat16)
     values = values_sum.astype(jnp.bfloat16)
+
+    def _find_series(x_in):
+        h_now = jnp.stack([x_in for _ in range(jax.lax.psum(1, TOK))], axis=0)
+        arr_out = jax.lax.all_to_all(h_now, TOK, 0, 0)
+        new = jnp.concatenate(arr_out, 1)
+        return new
+
     query_full, input_full, hidden_full, mixkey_full, colour_full = (
         *in_one_piece((query_weight, gru_input, gru_hidden, mix_key), TOK, 0, 1),
-        lax.all_gather(render_out, TOK, axis=1, tiled=True),
+        _find_series(render_out),
     )
     slots = slots_init
     for step in range(ITERS):

time: 694 us -> 667 us (0.961)
  blocking collectives: 341 us -> 298 us
  starting transfers between devices: 51.1 us -> 61.4 us
    all_gather x1 -> x0, blocking collectives: 43.3 us -> none  [on_device(): lax.all_gather(render_out, TOK, axis=1, tiled=True)]
    unnamed x34 -> x33, local copies, waits for them, and re-layouts: 18.9 us -> 18.8 us
  transfers between devices with their start and end apart: 12 -> 13, of which waited for: 8 -> 10; matrix products, arithmetic and copies ran while one was open for 6% -> 7% of each run, Pallas kernels for 0% -> 0%
where the time goes in v1:
time: 667 us; the launch traced here: 664 us
  blocking collectives  298 us (45%)
  waiting for transfers between devices  171 us (26%)
  local copies, waits for them, and re-layouts  64.8 us (10%)
  starting transfers between devices  61.4 us (9%)
  matrix products  41.2 us (6%)
  between operations  17.9 us (3%)
  other arithmetic  9.31 us (1%)
    all_gather x2, waiting for transfers between devices, in_one_piece(): lax.all_gather(both, axis, axis=dim, tiled=True)  127 us
    all_to_all x4, blocking collectives, summed_on_arrival(): parts = lax.all_to_all(in_blocks(value, dim, size), axis, 0, 0, tiled=True)  88.5 us
    psum x4, blocking collectives, by_axis(): value = lax.psum(value, axis)  68.5 us
    all_gather x2, blocking collectives, gather_in_order(): parts = lax.all_gather(parts, axes[k], axis=0, tiled=True)  58 us
    all_to_all x3, blocking collectives, sum_in_two_steps(): lax.all_to_all(nearer, far, split_axis=0, concat_axis=0, tiled=True)  57.7 us
    all_to_all x8, starting transfers between devices, from_everyone(): lax.all_to_all(jnp.broadcast_to(value[None], (size, *value.shape)), axis,...  47.9 us
    all_to_all x8, waiting for transfers between devices, from_everyone(): lax.all_to_all(jnp.broadcast_to(value[None], (size, *value.shape)), axis,...  39.7 us
    all_to_all x2, blocking collectives, from_everyone(): lax.all_to_all(jnp.broadcast_to(value[None], (size, *value.shape)), axis,...  25.3 us
  transfers between devices with their start and end apart: 13, of which 10 were waited for; matrix products, arithmetic and copies ran while one was open for 7% of the time, Pallas kernels for 0%

profile of v1, /device:TPU:32, one launch (start us, length us, event | category | flops | bytes accessed | tf_op | source)
XLA Modules:
  0.0 663.7 jit_solution(1991844985618394575)
XLA Ops:
  13.0 11.8 %all-to-all-start = ((bf16[64,8,768]{2,1,0:T(8,128)(2,1)}), bf16[64,8,768]{2,1,0:T(8,128)(2,1)S(1)}, u32[]{:S(2)}, u32[]{:S(2)}) async-start(bf16[64,8,768]{2,1,0:T(8,128)(2,1)} %broadcast_in_dim.28), calls=%async_computation | async-start | bytes 1572864 | tf_op jit(solution)/shard_map/all_to_all | solution.py:16
  25.1 23.2 %all-to-all-done = bf16[64,8,768]{2,1,0:T(8,128)(2,1)S(1)} async-done(((bf16[64,8,768]{2,1,0:T(8,128)(2,1)}), bf16[64,8,768]{2,1,0:T(8,128)(2,1)S(1)}, u32[]{:S(2)}, u32[]{:S(2)}) %all-to-all-start) | async-done | bytes 786464 | tf_op jit(solution)/shard_map/all_to_all | solution.py:16
  49.0 43.4 %all-gather.10.cloned.1.call-done = bf16[64,12,1536]{2,1,0:T(8,128)(2,1)} async-done(((bf16[1,12,1536]{2,1,0:T(8,128)(2,1)}), bf16[64,12,1536]{2,1,0:T(8,128)(2,1)}) %all-gather.10.cloned.1.call-update) | async-done | bytes 2359312 | tf_op jit(solution)/shard_map/all_gather | solution.py:34
  92.4 4.9 reshape.153
  99.8 83.6 %all-gather.12.cloned.1.call-done = bf16[64,12,6144]{2,1,0:T(8,128)(2,1)} async-done(((bf16[1,12,6144]{2,1,0:T(8,128)(2,1)}), bf16[64,12,6144]{2,1,0:T(8,128)(2,1)}) %all-gather.12.cloned.1.call-update) | async-done | bytes 9437200 | tf_op jit(solution)/shard_map/all_gather | solution.py:34
  183.4 13.7 %reshape.155 = bf16[768,6144]{1,0:T(8,128)(2,1)} reshape(bf16[64,12,6144]{2,1,0:T(8,128)(2,1)} %all-gather.12.cloned.1.call-done) | data formatting | bytes 18874368
  199.9 10.9 %all_to_all.110 = f32[8,32,193]{2,1,0:T(8,128)S(1)} all-to-all(f32[8,32,193]{2,1,0:T(8,128)S(1)} %copy.53), channel_id=1, replica_groups=mesh['tok_0'=8,'tok_1'=4,'tok_2'=2,'rep'=4] {'tok_2','rep'}, dimensions={0} | all-to-all | bytes 395264 | tf_op jit(solution)/shard_map/all_to_all | solution.py:49
  210.9 14.4 %all_to_all.111 = f32[32,1,193]{2,1,0:T(1,128)S(1)} all-to-all(f32[32,1,193]{2,1,0:T(1,128)S(1)} %all_to_all.71), channel_id=1, replica_groups=mesh['tok_0'=8,'tok_1'=4,'tok_2'=2,'rep'=4] {'tok_0','tok_1'}, dimensions={0} | all-to-all | bytes 49408 | tf_op jit(solution)/shard_map/all_to_all | solution.py:57
  225.3 12.7 %all_to_all.112 = f32[32,1,193]{2,1,0:T(1,128)S(1)} all-to-all(f32[32,1,193]{2,1,0:T(1,128)S(1)} %broadcast_in_dim.29), channel_id=1, replica_groups=mesh['tok_0'=8,'tok_1'=4,'tok_2'=2,'rep'=4] {'tok_0','tok_1'}, dimensions={0} | all-to-all | bytes 49408 | tf_op jit(solution)/shard_map/all_to_all | solution.py:16
  238.8 3.4 all-to-all-start.4
  244.9 4.1 all-to-all-done.4
  249.6 2.8 fusion.9
  255.6 9.7 %all_to_all.113 = f32[8,32,193]{2,1,0:T(8,128)S(1)} all-to-all(f32[8,32,193]{2,1,0:T(8,128)S(1)} %copy.55), channel_id=1, replica_groups=mesh['tok_0'=8,'tok_1'=4,'tok_2'=2,'rep'=4] {'tok_2','rep'}, dimensions={0} | all-to-all | bytes 395264 | tf_op jit(solution)/shard_map/all_to_all | solution.py:49
  265.4 12.8 %all_to_all.114 = f32[32,1,193]{2,1,0:T(1,128)S(1)} all-to-all(f32[32,1,193]{2,1,0:T(1,128)S(1)} %all_to_all.76), channel_id=1, replica_groups=mesh['tok_0'=8,'tok_1'=4,'tok_2'=2,'rep'=4] {'tok_0','tok_1'}, dimensions={0} | all-to-all | bytes 49408 | tf_op jit(solution)/shard_map/all_to_all | solution.py:57
  278.3 12.7 %all_to_all.115 = f32[32,1,193]{2,1,0:T(1,128)S(1)} all-to-all(f32[32,1,193]{2,1,0:T(1,128)S(1)} %broadcast_in_dim.32), channel_id=1, replica_groups=mesh['tok_0'=8,'tok_1'=4,'tok_2'=2,'rep'=4] {'tok_0','tok_1'}, dimensions={0} | all-to-all | bytes 49408 | tf_op jit(solution)/shard_map/all_to_all | solution.py:16
  291.7 3.5 all-to-all-start.8
  295.2 2.7 fusion.2
  298.0 4.1 all-to-all-done.8
  302.7 5.4 all-to-all-start.15
  308.7 2.8 fusion.7
  317.3 9.9 %all_to_all.116 = f32[8,32,193]{2,1,0:T(8,128)} all-to-all(f32[8,32,193]{2,1,0:T(8,128)S(1)} %copy.57), channel_id=1, replica_groups=mesh['tok_0'=8,'tok_1'=4,'tok_2'=2,'rep'=4] {'tok_2','rep'}, dimensions={0} | all-to-all | bytes 395264 | tf_op jit(solution)/shard_map/all_to_all | solution.py:49
  328.6 7.6 %all-to-all-start.13 = ((bf16[32,12,1536]{2,1,0:T(8,128)(2,1)}), bf16[32,12,1536]{2,1,0:T(8,128)(2,1)S(1)}, u32[]{:S(2)}, u32[]{:S(2)}) async-start(bf16[32,12,1536]{2,1,0:T(8,128)(2,1)} %broadcast_in_dim.39), calls=%async_computation.13 | async-start | bytes 3145728 | tf_op jit(solution)/shard_map/all_to_all | solution.py:16
  336.2 12.7 %all-gather.3 = bf16[4,12,768]{2,1,0:T(8,128)(2,1)S(1)} all-gather(bf16[1,12,768]{2,1,0:T(8,128)(2,1)S(1)} %bitcast.69), channel_id=2, replica_groups=mesh['tok_0'=8,'tok_1'=4,'tok_2'=2,'rep'=4] {'tok_1'}, dimensions={0}, use_global_device_ids=true | all-gather | bytes 92160 | tf_op jit(solution)/shard_map/all_gather | solution.py:94
  348.9 45.4 %all_gather.18 = bf16[32,12,768]{2,1,0:T(8,128)(2,1)S(1)} all-gather(bf16[4,12,768]{2,1,0:T(8,128)(2,1)S(1)} %all-gather.3), channel_id=1, replica_groups=mesh['tok_0'=8,'tok_1'=4,'tok_2'=2,'rep'=4] {'tok_0'}, dimensions={0}, use_global_device_ids=true | all-gather | bytes 663552 | tf_op jit(solution)/shard_map/all_gather | solution.py:94
  396.9 7.9 %all-to-all-start.10 = ((f32[32,1,193]{2,1,0:T(1,128)}), f32[32,1,193]{2,1,0:T(1,128)S(1)}, u32[]{:S(2)}, u32[]{:S(2)}) async-start(f32[32,1,193]{2,1,0:T(1,128)} %all_to_all.81), calls=%async_computation.10 | async-start | bytes 65536 | tf_op jit(solution)/shard_map/all_to_all | solution.py:57
  407.1 3.2 reshape.147
  410.3 3.1 copy.73
  413.4 3.1 reshape_reshape.33
  418.2 2.9 broadcast_in_dim.40
  421.1 3.9 all-to-all-start.14
  425.1 3.0 all-to-all-done.14
  428.8 10.1 %all-to-all-start.11 = ((f32[32,1,193]{2,1,0:T(1,128)}), f32[32,1,193]{2,1,0:T(1,128)S(1)}, u32[]{:S(2)}, u32[]{:S(2)}) async-start(f32[32,1,193]{2,1,0:T(1,128)} %broadcast_in_dim.35), calls=%async_computation.11 | async-start | bytes 65536 | tf_op jit(solution)/shard_map/all_to_all | solution.py:16
  441.2 3.0 copy.62
  448.4 4.3 all-to-all-start.12
  455.4 4.1 all-to-all-done.12
  460.1 2.8 fusion.5
  465.9 3.6 fusion.31
  471.1 5.0 fusion.12
  476.1 7.9 %reshape_reshape.35 = f32[32,8,3,1536]{3,2,1,0:T(4,128)} reshape(f32[768,1536]{1,0:T(8,128)} %fusion.12) | data formatting | bytes 9437184 | tf_op jit(solution)/shard_map/reshape;reshape | solution.py:43
  484.0 5.5 copy.64
  489.5 57.9 %all_to_all.117 = f32[8,32,3,1536]{3,1,2,0:T(8,128)} all-to-all(f32[8,32,3,1536]{3,1,2,0:T(8,128)S(1)} %copy.64), channel_id=1, replica_groups=mesh['tok_0'=8,'tok_1'=4,'tok_2'=2,'rep'=4] {'tok_2','rep'}, dimensions={0} | all-to-all | bytes 9437184 | tf_op jit(solution)/shard_map/all_to_all | solution.py:49
  547.4 2.8 reduce_sum.238
  550.5 30.5 %all_to_all.118 = f32[32,3,1536]{2,1,0:T(4,128)S(1)} all-to-all(f32[32,3,1536]{2,1,0:T(4,128)S(1)} %copy.65), channel_id=1, replica_groups=mesh['tok_0'=8,'tok_1'=4,'tok_2'=2,'rep'=4] {'tok_0','tok_1'}, dimensions={0} | all-to-all | bytes 1179648 | tf_op jit(solution)/shard_map/all_to_all | solution.py:57
  581.8 3.3 all-to-all-start.18
  585.3 27.7 %all-reduce = (f32[]{:T(128)}, f32[3,1536]{1,0:T(4,128)S(1)}) all-reduce(f32[]{:T(128)} %get-tuple-element.18, f32[3,1536]{1,0:T(4,128)S(1)} %fusion.145), channel_id=1, replica_groups=mesh['tok_0'=8,'tok_1'=4,'tok_2'=2,'rep'=4] {'tok_0'}, use_global_device_ids=true, to_apply=%region_26.27 | all-reduce | flops 4609 | bytes 36872 | tf_op jit(solution)/shard_map/psum | solution.py:107
  613.1 17.6 %all-reduce.2 = (f32[]{:T(128)}, f32[3,1536]{1,0:T(4,128)S(1)}) all-reduce(f32[]{:T(128)} %get-tuple-element.5, f32[3,1536]{1,0:T(4,128)S(1)} %get-tuple-element.6), channel_id=1, replica_groups=mesh['tok_0'=8,'tok_1'=4,'tok_2'=2,'rep'=4] {'tok_1'}, use_global_device_ids=true, to_apply=%region_27.28 | all-reduce | flops 4609 | bytes 36872 | tf_op jit(solution)/shard_map/psum | solution.py:107
  630.7 4.5 all-reduce.3
  635.2 18.7 %all-reduce.1 = (f32[]{:T(128)}, f32[3,1536]{1,0:T(4,128)}) all-reduce(f32[]{:T(128)} %get-tuple-element.11, f32[3,1536]{1,0:T(4,128)S(1)} %get-tuple-element.12), channel_id=1, replica_groups=mesh['tok_0'=8,'tok_1'=4,'tok_2'=2,'rep'=4] {'rep'}, use_global_device_ids=true, to_apply=%region_29.30 | all-reduce | flops 4609 | bytes 36872 | tf_op jit(solution)/shard_map/psum | solution.py:107
  (140 shorter events, 51.3 us)
Async XLA Ops:
  8.0 16.7 %copy-start.3 = (f32[64,768]{1,0:T(8,128)S(1)}, f32[64,768]{1,0:T(8,128)}, u32[]{:S(2)}) copy-start(f32[64,768]{1,0:T(8,128)} %param.22) | copy-start | bytes 589828
  8.0 40.3 %copy-start.11 = (s32[256]{0:T(256)S(1)}, s32[256]{0:T(256)}, u32[]{:S(2)}) copy-start(s32[256]{0:T(256)} %param.17) | copy-start | bytes 3076
  8.0 40.2 %copy-start.6 = (bf16[256,768]{1,0:T(8,128)(2,1)S(1)}, bf16[256,768]{1,0:T(8,128)(2,1)}, u32[]{:S(2)}) copy-start(bf16[256,768]{1,0:T(8,128)(2,1)} %param.16) | copy-start | bytes 1179652
  8.0 84.4 %all-gather.10.cloned.1.call-start = ((), (), s32[]{:S(2)}) async-start(), calls=%async_computation.20 | async-start | bytes 3194880 | tf_op jit(solution)/shard_map/all_gather | solution.py:34
  9.6 173.8 %all-gather.12.cloned.1.call-start = ((), (), s32[]{:S(2)}) async-start(), calls=%async_computation.21 | async-start | bytes 12779520 | tf_op jit(solution)/shard_map/all_gather | solution.py:34
  13.0 35.3 %all-to-all-start = ((bf16[64,8,768]{2,1,0:T(8,128)(2,1)}), bf16[64,8,768]{2,1,0:T(8,128)(2,1)S(1)}, u32[]{:S(2)}, u32[]{:S(2)}) async-start(bf16[64,8,768]{2,1,0:T(8,128)(2,1)} %broadcast_in_dim.28), calls=%async_computation | async-start | bytes 1572864 | tf_op jit(solution)/shard_map/all_to_all | solution.py:16
  97.3 2.0 copy-start.4
  99.8 153.0 %copy-start.13 = (bf16[256,768]{1,0:T(8,128)(2,1)}, bf16[256,768]{1,0:T(8,128)(2,1)S(1)}, u32[]{:S(2)}) copy-start(bf16[256,768]{1,0:T(8,128)(2,1)S(1)} %convolution_convert_fusion.1) | copy-start | bytes 1179652
  238.8 10.2 %all-to-all-start.4 = ((f32[8,32,193]{2,1,0:T(8,128)}), f32[8,32,193]{2,1,0:T(8,128)S(1)}, u32[]{:S(2)}, u32[]{:S(2)}) async-start(f32[8,32,193]{2,1,0:T(8,128)} %broadcast_in_dim.31), calls=%async_computation.4 | async-start | bytes 524288 | tf_op jit(solution)/shard_map/all_to_all | solution.py:16
  291.7 10.4 %copy-start.12 = (bf16[3,24]{1,0:T(4,128)(2,1)S(1)}, bf16[3,24]{1,0:T(4,128)(2,1)}, u32[]{:S(2)}) copy-start(bf16[3,24]{1,0:T(4,128)(2,1)} %param.31) | copy-start | bytes 436
  291.7 10.4 %all-to-all-start.8 = ((f32[8,32,193]{2,1,0:T(8,128)}), f32[8,32,193]{2,1,0:T(8,128)S(1)}, u32[]{:S(2)}, u32[]{:S(2)}) async-start(f32[8,32,193]{2,1,0:T(8,128)} %broadcast_in_dim.34), calls=%async_computation.8 | async-start | bytes 524288 | tf_op jit(solution)/shard_map/all_to_all | solution.py:16
  302.7 14.6 %all-to-all-start.15 = ((bf16[64,3,24]{2,1,0:T(4,128)(2,1)}), bf16[64,3,24]{2,1,0:T(4,128)(2,1)S(1)}, u32[]{:S(2)}, u32[]{:S(2)}) async-start(bf16[64,3,24]{2,1,0:T(4,128)(2,1)} %stack.2), calls=%async_computation.15 | async-start | bytes 131072 | tf_op jit(solution)/shard_map/all_to_all | solution.py:172
  312.0 15.3 %copy-start.7 = (bf16[12,1536]{1,0:T(8,128)(2,1)S(1)}, bf16[12,1536]{1,0:T(8,128)(2,1)}, u32[]{:S(2)}) copy-start(bf16[12,1536]{1,0:T(8,128)(2,1)} %param.30) | copy-start | bytes 110596
  327.3 9.0 %copy-start.8 = (bf16[12,768]{1,0:T(8,128)(2,1)S(1)}, bf16[12,768]{1,0:T(8,128)(2,1)}, u32[]{:S(2)}) copy-start(bf16[12,768]{1,0:T(8,128)(2,1)} %param.28) | copy-start | bytes 55300
  328.6 68.3 %all-to-all-start.13 = ((bf16[32,12,1536]{2,1,0:T(8,128)(2,1)}), bf16[32,12,1536]{2,1,0:T(8,128)(2,1)S(1)}, u32[]{:S(2)}, u32[]{:S(2)}) async-start(bf16[32,12,1536]{2,1,0:T(8,128)(2,1)} %broadcast_in_dim.39), calls=%async_computation.13 | async-start | bytes 3145728 | tf_op jit(solution)/shard_map/all_to_all | solution.py:16
  336.2 70.9 %all-gather.8.cloned.1.call-start = ((), (), s32[]{:S(2)}) async-start(), calls=%async_computation.19 | async-start | bytes 1769472 | tf_op jit(solution)/shard_map/all_gather | solution.py:94
  396.9 21.3 %all-to-all-start.10 = ((f32[32,1,193]{2,1,0:T(1,128)}), f32[32,1,193]{2,1,0:T(1,128)S(1)}, u32[]{:S(2)}, u32[]{:S(2)}) async-start(f32[32,1,193]{2,1,0:T(1,128)} %all_to_all.81), calls=%async_computation.10 | async-start | bytes 65536 | tf_op jit(solution)/shard_map/all_to_all | solution.py:57
  421.1 17.8 %copy-start.10 = (s32[256]{0:T(256)S(1)}, s32[256]{0:T(256)}, u32[]{:S(2)}) copy-start(s32[256]{0:T(256)} %param.19) | copy-start | bytes 3076
  421.1 7.0 %all-to-all-start.14 = ((bf16[2,32,12,1536]{3,1,2,0:T(8,128)(2,1)}), bf16[2,32,12,1536]{3,1,2,0:T(8,128)(2,1)S(1)}, u32[]{:S(2)}, u32[]{:S(2)}) async-start(bf16[2,32,12,1536]{3,1,2,0:T(8,128)(2,1)} %broadcast_in_dim.40), calls=%async_computation.14 | async-start | bytes 4718592 | tf_op jit(solution)/shard_map/all_to_all | solution.py:16
  428.1 13.1 %copy-start = (bf16[2,32,12,1536]{3,1,2,0:T(8,128)(2,1)}, bf16[2,32,12,1536]{3,1,2,0:T(8,128)(2,1)S(1)}, u32[]{:S(2)}) copy-start(bf16[2,32,12,1536]{3,1,2,0:T(8,128)(2,1)S(1)} %all-to-all-done.14) | copy-start | bytes 7077892
  428.8 18.9 %all-to-all-start.11 = ((f32[32,1,193]{2,1,0:T(1,128)}), f32[32,1,193]{2,1,0:T(1,128)S(1)}, u32[]{:S(2)}, u32[]{:S(2)}) async-start(f32[32,1,193]{2,1,0:T(1,128)} %broadcast_in_dim.35), calls=%async_computation.11 | async-start | bytes 65536 | tf_op jit(solution)/shard_map/all_to_all | solution.py:16
  448.4 11.1 %all-to-all-start.12 = ((f32[8,32,193]{2,1,0:T(8,128)}), f32[8,32,193]{2,1,0:T(8,128)S(1)}, u32[]{:S(2)}, u32[]{:S(2)}) async-start(f32[8,32,193]{2,1,0:T(8,128)} %broadcast_in_dim.37), calls=%async_computation.12 | async-start | bytes 524288 | tf_op jit(solution)/shard_map/all_to_all | solution.py:16
  462.9 2.0 copy-start.1
  462.9 2.0 copy-start.2
  463.1 2.8 copy-start.5
  465.9 3.6 copy-start.9
  581.8 72.7 %all-to-all-start.18 = ((f32[4,3,1536]{2,1,0:T(4,128)}), f32[4,3,1536]{2,1,0:T(4,128)S(1)}, u32[]{:S(2)}, u32[]{:S(2)}) async-start(f32[4,3,1536]{2,1,0:T(4,128)} %broadcast_in_dim.41), calls=%async_computation.18 | async-start | bytes 196608 | tf_op jit(solution)/shard_map/all_to_all | solution.py:16
Sparse Core Ops, SparseCore 0:
  12.2 80.1 all-gather.9
  95.7 87.6 all-gather.11
Sparse Core Ops, SparseCore 1:
  395.4 11.6 all-gather.7
